TPU v7x, 32 devices: a whole 2x2x4 slice. The times are simulated.
32 devices in a mesh: chan: 4 (over y, x), space: 4 (over z), rep: 2 (over core).
Axes of the slice: x: 2, y: 2, z: 4, core: 2. Of those that a mesh axis runs over, the one named last changes fastest.
Arguments:
- inputs: bfloat16 [2, 2, 16, 512, 128], P('rep', None, 'space', 'chan'), may hold values from -6 to 6
- grad_out: bfloat16 [2, 2, 16, 512, 128], P('rep', None, 'space', 'chan'), may hold values from -6 to 6
- weight: bfloat16 [3, 3, 3, 512, 512], P(None, None, None, 'chan'), may hold values from -0.0546875 to 0.0546875
Outputs:
- grad_in: bfloat16 [2, 2, 16, 512, 128], P('rep', None, 'space', 'chan')
- grad_weight: float32 [3, 3, 3, 512, 512], P(None, None, None, ('chan', 'rep'))
All inputs are finite; a program needn't handle non-finite values.
Results may differ from a plain program's by a relative error of at most 0.0031.
Values may be sent and summed in bfloat16 or wider, within the bound.
A program may use at most 64 MiB of HBM per device.

v0:
```python
import jax
import jax.numpy as jnp
from jax import lax
from jax.sharding import PartitionSpec as P


def with_halo(cells, sides, width):
    for axis, dim in sides:
        count = lax.axis_size(axis)
        ends = count - 1
        head = lax.slice_in_dim(cells, 0, width, axis=dim)
        tail = lax.slice_in_dim(cells, cells.shape[dim] - width, cells.shape[dim], axis=dim)
        cells = jnp.concatenate(
            [
                lax.ppermute(tail, axis, [(i, (i + 1) % count) for i in range(ends)]),
                cells,
                lax.ppermute(head, axis, [((i + 1) % count, i) for i in range(ends)]),
            ],
            axis=dim,
        )
    return cells


def silu_slope(values):
    logistic = jax.nn.sigmoid(values)
    return logistic * (1.0 + values * (1.0 - logistic))


def tap_windows(padded, frame_count, row_count, col_count):
    windows = []
    for frame_tap in range(3):
        for row_tap in range(3):
            for col_tap in range(3):
                windows.append(
                    padded[
                        :,
                        2 - frame_tap : 2 - frame_tap + frame_count,
                        2 - row_tap : 2 - row_tap + row_count,
                        :,
                        2 - col_tap : 2 - col_tap + col_count,
                    ]
                )
    return jnp.concatenate(windows, axis=3)


def on_device(inputs, grad_out, weight):
    clip_count, frame_count, row_count, in_part, col_count = inputs.shape
    out_part = grad_out.shape[3]
    gathered = lax.all_gather(inputs, "chan", axis=3, tiled=True)
    activated = jax.nn.silu(gathered.astype(jnp.float32)).astype(jnp.bfloat16)
    in_width = activated.shape[3]
    grad_rim = with_halo(grad_out, (("space", 2),), 1)
    grad_pad = jnp.pad(grad_rim, ((0, 0), (0, 2), (0, 0), (0, 0), (1, 1)))
    stacked = tap_windows(grad_pad, frame_count, row_count, col_count)
    local_flat = jnp.einsum(
        "cthkw,cthiw->ki", stacked, activated, preferred_element_type=jnp.float32
    )
    local_weight = local_flat.reshape(3, 3, 3, out_part, in_width)
    clip_summed = lax.psum_scatter(local_weight, "rep", scatter_dimension=3, tiled=True)
    summed = lax.psum(clip_summed, "space")
    grad_weight = summed * (1.0 / 256.0)
    flat_kernel = weight.reshape(27 * out_part, weight.shape[4])
    partial_value = jnp.einsum(
        "cthkw,ki->cthiw", stacked, flat_kernel, preferred_element_type=jnp.float32
    )
    active_grad = lax.psum_scatter(partial_value, "chan", scatter_dimension=3, tiled=True)
    grad_in = (active_grad * silu_slope(inputs.astype(jnp.float32))).astype(jnp.bfloat16)
    return (grad_in, grad_weight)


def solution(mesh):
    return jax.shard_map(
        on_device,
        mesh=mesh,
        in_specs=(
            P("rep", None, "space", "chan", None),
            P("rep", None, "space", "chan", None),
            P(None, None, None, "chan", None),
        ),
        out_specs=(
            P("rep", None, "space", "chan", None),
            P(None, None, None, ("chan", "rep"), None),
        ),
        check_vma=False,
    )
```

profile of v0, /device:TPU:0, one launch (start us, length us, event | category | flops | bytes accessed | tf_op | source)
XLA Modules:
  0.0 258.9 jit_solution(6788880601391279087)
XLA Ops:
  7.2 0.0 copy-start
  7.2 0.0 all-gather.2.cloned.1.call-start
  7.2 1.9 copy.15
  9.2 1.5 fusion.32
  10.7 1.3 collective-permute-start.1
  12.0 6.2 %collective-permute-start = (bf16[1,2,1,128,128]{3,4,2,1,0:T(8,128)(2,1)}, bf16[1,2,1,128,128]{3,4,2,1,0:T(8,128)(2,1)}, u32[]{:S(2)}, u32[]{:S(2)}) collective-permute-start(bf16[1,2,1,128,128]{3,4,2,1,0:T(8,128)(2,1)} %get-tuple-element.6), channel_id=1, source_target_pairs={{0,2},{2,4},{4,6},{1,3},{3,5},{5,7},{8,10},{10,12},{12,14},{9,11},... | collective-permute-start | bytes 196616 | tf_op jit(solution)/shard_map/ppermute | solution.py:15
  18.2 0.0 all-gather.2.cloned.1.call-update
  18.2 0.0 reduce-scatter.5.cloned.1.call-start
  18.2 0.0 copy-start.1
  18.3 0.1 broadcast_dynamic-update-slice_fusion.6
  18.4 0.1 broadcast_dynamic-update-slice_fusion.5
  18.5 0.1 broadcast_dynamic-update-slice_fusion.4
  18.6 0.1 broadcast_dynamic-update-slice_fusion.3
  18.7 0.1 broadcast_dynamic-update-slice_fusion.2
  18.8 0.1 broadcast_dynamic-update-slice_fusion.1
  18.9 0.1 broadcast_dynamic-update-slice_fusion
  19.0 0.1 broadcast_dynamic-update-slice_fusion.8
  19.1 0.0 collective-permute-done.1
  19.1 0.6 collective-permute-done
  19.7 1.2 fusion.20
  20.9 0.1 slice_dynamic-update-slice_fusion.14
  21.0 0.1 slice_dynamic-update-slice_fusion.13
  21.2 0.1 slice_dynamic-update-slice_fusion.12
  21.2 0.1 slice_dynamic-update-slice_fusion.11
  21.3 0.1 slice_dynamic-update-slice_fusion.10
  21.5 0.1 slice_dynamic-update-slice_fusion.9
  21.6 0.1 slice_dynamic-update-slice_fusion.8
  21.7 0.1 slice_dynamic-update-slice_fusion.7
  21.8 0.1 slice_dynamic-update-slice_fusion.6
  21.9 0.1 slice_dynamic-update-slice_fusion.5
  22.0 0.0 copy-done.1
  22.0 0.9 fusion.31
  22.9 0.1 slice_dynamic-update-slice_fusion.4
  23.0 0.1 slice_dynamic-update-slice_fusion.3
  23.1 0.1 constant_dynamic-update-slice_fusion
  23.2 0.1 slice_dynamic-update-slice_fusion.2
  23.3 0.1 slice_dynamic-update-slice_fusion.1
  23.4 0.9 fusion.30
  24.3 0.1 slice_dynamic-update-slice_fusion
  24.4 0.0 copy-start.2
  24.4 2.9 %copy-done.2 = bf16[1,2,4,3456,128]{3,4,2,1,0:T(8,128)(2,1)} copy-done((bf16[1,2,4,3456,128]{3,4,2,1,0:T(8,128)(2,1)}, bf16[1,2,4,3456,128]{3,4,2,1,0:T(8,128)(2,1)S(1)}, u32[]{:S(2)}) %copy-start.2) | copy-done | bytes 7077912
  27.3 10.2 %copy.22 = bf16[3456,4,2,128]{3,0,2,1:T(8,128)(2,1)} copy(bf16[3456,4,2,128]{0,3,1,2:T(8,128)(2,1)} %bitcast.31) | data formatting | bytes 14155776 | tf_op jit(solution)/shard_map/cthkw,cthiw->ki/dot_general | solution.py:55
  37.5 8.1 %all-gather.2.cloned.1.call-done = bf16[1,2,4,512,128]{4,3,2,1,0:T(8,128)(2,1)} async-done(((bf16[1,2,4,128,128]{4,3,2,1,0:T(8,128)(2,1)}), bf16[1,2,4,512,128]{4,3,2,1,0:T(8,128)(2,1)}) %all-gather.2.cloned.1.call-update) | async-done | bytes 1048592 | tf_op jit(solution)/shard_map/all_gather | solution.py:49
  45.6 6.6 %fusion = f32[3,3,3,128,512,1,1]{4,3,0,1,2,6,5:T(8,128)S(1)} fusion(bf16[3,3,3,128,4,2,128]{6,3,2,1,0,5,4:T(8,128)(2,1)} %bitcast.32, bf16[1,2,4,512,128]{4,3,2,1,0:T(8,128)(2,1)} %all-gather.2.cloned.1.call-done), kind=kOutput, calls=%fused_computation | convolution fusion | flops 3627024384 | bytes 15204352 | tf_op jit(solution)/shard_map/cthkw,cthiw->ki/dot_general | solution.py:55
  52.3 3.7 %copy.38 = f32[3,3,3,128,512,1,1]{4,3,2,1,0,5,6:T(8,128)} copy(f32[3,3,3,128,512,1,1]{4,3,0,1,2,6,5:T(8,128)S(1)} %fusion) | data formatting | bytes 14155776 | tf_op jit(solution)/shard_map/cthkw,cthiw->ki/dot_general | solution.py:55
  56.0 0.0 reduce-scatter.5.cloned.1.call-update
  56.0 0.0 reduce-scatter.3.cloned.1.call-start
  56.1 0.0 copy-done
  56.1 7.5 %fusion.13 = f32[1,2,4,512,128]{3,4,2,1,0:T(8,128)} fusion(bf16[3456,512,1,1]{1,0,3,2:T(8,128)(2,1)S(1)} %bitcast.29, bf16[1,2,4,3456,128]{3,4,2,1,0:T(8,128)(2,1)} %copy-done.2), kind=kOutput, calls=%fused_computation.20 | convolution fusion | flops 3623878656 | bytes 12713984 | tf_op jit(solution)/shard_map/cthkw,ki->cthiw/dot_general | solution.py:63
  63.6 0.0 reduce-scatter.3.cloned.1.call-update
  63.7 0.0 all-reduce.3.cloned.1.call-start
  63.7 7.9 %reduce-scatter.5.cloned.1.call-done = f32[3,3,3,64,512]{4,3,2,1,0:T(8,128)} async-done(((f32[3,3,3,128,512]{4,3,2,1,0:T(8,128)}), f32[3,3,3,64,512]{4,3,2,1,0:T(8,128)}) %reduce-scatter.5.cloned.1.call-update) | async-done | bytes 3538960 | tf_op jit(solution)/shard_map/reduce_scatter | solution.py:59
  71.6 0.0 all-reduce.3.cloned.1.call-update
  71.7 1.8 copy.21
  73.5 38.5 %reduce-scatter.3.cloned.1.call-done = f32[1,2,4,128,128]{3,4,2,1,0:T(8,128)} async-done(((f32[1,2,4,512,128]{3,4,2,1,0:T(8,128)}), f32[1,2,4,128,128]{3,4,2,1,0:T(8,128)}) %reduce-scatter.3.cloned.1.call-update) | async-done | bytes 524304 | tf_op jit(solution)/shard_map/reduce_scatter | solution.py:66
  111.9 2.0 fusion.29
  113.9 1.8 copy.25
  115.7 132.2 %all-reduce.3.cloned.1.call-done = f32[3,3,3,64,512]{4,3,2,1,0:T(8,128)} async-done(((f32[3,3,3,64,512]{4,3,2,1,0:T(8,128)}), f32[3,3,3,64,512]{4,3,2,1,0:T(8,128)}) %all-reduce.3.cloned.1.call-update) | async-done | bytes 3538960 | tf_op jit(solution)/shard_map/psum | solution.py:60
  248.0 4.4 %broadcast_multiply_fusion = f32[3,3,3,64,512]{4,3,2,1,0:T(8,128)} fusion(f32[3,3,3,64,512]{4,3,2,1,0:T(8,128)} %all-reduce.3.cloned.1.call-done), kind=kLoop, calls=%fused_computation.13 | loop fusion | flops 884736 | bytes 7077888 | tf_op jit(solution)/shard_map/mul | solution.py:61
  (1 shorter events, 0.0 us)
Async XLA Ops:
  7.2 48.9 %copy-start = (bf16[3,3,3,128,512]{4,3,2,1,0:T(8,128)(2,1)S(1)}, bf16[3,3,3,128,512]{4,3,2,1,0:T(8,128)(2,1)}, u32[]{:S(2)}) copy-start(bf16[3,3,3,128,512]{4,3,2,1,0:T(8,128)(2,1)} %param.5) | copy-start | bytes 10616836
  7.2 38.5 %all-gather.2.cloned.1.call-start = ((), (), s32[]{:S(2)}) async-start(), calls=%async_computation.3 | async-start | bytes 1310720 | tf_op jit(solution)/shard_map/all_gather | solution.py:49
  10.7 8.5 %collective-permute-start.1 = (bf16[1,2,1,128,128]{3,4,2,1,0:T(8,128)(2,1)}, bf16[1,2,1,128,128]{3,4,2,1,0:T(8,128)(2,1)}, u32[]{:S(2)}, u32[]{:S(2)}) collective-permute-start(bf16[1,2,1,128,128]{3,4,2,1,0:T(8,128)(2,1)} %get-tuple-element.7), channel_id=1, source_target_pairs={{2,0},{4,2},{6,4},{3,1},{5,3},{7,5},{10,8},{12,10},{14,12},{11,9},... | collective-permute-start | bytes 196616 | tf_op jit(solution)/shard_map/ppermute | solution.py:17
  12.0 7.8 %collective-permute-start = (bf16[1,2,1,128,128]{3,4,2,1,0:T(8,128)(2,1)}, bf16[1,2,1,128,128]{3,4,2,1,0:T(8,128)(2,1)}, u32[]{:S(2)}, u32[]{:S(2)}) collective-permute-start(bf16[1,2,1,128,128]{3,4,2,1,0:T(8,128)(2,1)} %get-tuple-element.6), channel_id=1, source_target_pairs={{0,2},{2,4},{4,6},{1,3},{3,5},{5,7},{8,10},{10,12},{12,14},{9,11},... | collective-permute-start | bytes 196616 | tf_op jit(solution)/shard_map/ppermute | solution.py:15
  18.2 53.4 %reduce-scatter.5.cloned.1.call-start = ((), (), s32[]{:S(2)}) async-start(), calls=%async_computation.4 | async-start | bytes 10616832 | tf_op jit(solution)/shard_map/reduce_scatter | solution.py:59
  18.2 3.8 %copy-start.1 = (bf16[1,2,4,128,128]{3,4,2,1,0:T(8,128)(2,1)S(1)}, bf16[1,2,4,128,128]{3,4,2,1,0:T(8,128)(2,1)}, u32[]{:S(2)}) copy-start(bf16[1,2,4,128,128]{3,4,2,1,0:T(8,128)(2,1)} %copy.15) | copy-start | bytes 786436
  24.4 2.9 %copy-start.2 = (bf16[1,2,4,3456,128]{3,4,2,1,0:T(8,128)(2,1)}, bf16[1,2,4,3456,128]{3,4,2,1,0:T(8,128)(2,1)S(1)}, u32[]{:S(2)}) copy-start(bf16[1,2,4,3456,128]{3,4,2,1,0:T(8,128)(2,1)S(1)} %slice_dynamic-update-slice_fusion) | copy-start | bytes 21233668
  56.0 55.9 %reduce-scatter.3.cloned.1.call-start = ((), (), s32[]{:S(2)}) async-start(), calls=%async_computation.2 | async-start | bytes 2621440 | tf_op jit(solution)/shard_map/reduce_scatter | solution.py:66
  63.7 184.3 %all-reduce.3.cloned.1.call-start = ((), (), s32[]{:S(2)}) async-start(), calls=%async_computation.5 | async-start | bytes 7077888 | tf_op jit(solution)/shard_map/psum | solution.py:60
Sparse Core Ops, SparseCore 0:
  18.3 27.2 all-gather.1
  56.2 15.4 reduce-scatter.4
  75.5 36.4 reduce-scatter.2
  114.2 133.7 all-reduce.2
where the time goes:
time: 260 us; the launch traced here: 259 us
  waiting for transfers between devices  187 us (72%)
  local copies, waits for them, and re-layouts  26.3 us (10%)
  matrix products  14.2 us (5%)
  between operations  14 us (5%)
  other arithmetic  9.39 us (4%)
  starting transfers between devices  7.63 us (3%)
    psum x1, waiting for transfers between devices, on_device(): summed = lax.psum(clip_summed, 'space')  132 us
    reduce_scatter x1, waiting for transfers between devices, on_device(): lax.psum_scatter(partial_value, 'chan', scatter_dimension=3, tiled=True)  38.5 us
    dot_general x2, local copies, waits for them, and re-layouts, on_device(): jnp.einsum('cthkw,cthiw->ki', stacked, activated, preferred_element_type=...  14 us
    unnamed x33, local copies, waits for them, and re-layouts  10.7 us
    all_gather x1, waiting for transfers between devices, on_device(): gathered = lax.all_gather(inputs, 'chan', axis=3, tiled=True)  8.09 us
    reduce_scatter x1, waiting for transfers between devices, on_device(): lax.psum_scatter(local_weight, 'rep', scatter_dimension=3, tiled=True)  7.92 us
    dot_general x1, matrix products, on_device(): jnp.einsum('cthkw,ki->cthiw', stacked, flat_kernel, preferred_element_typ...  7.54 us
    dot_general x1, matrix products, on_device(): jnp.einsum('cthkw,cthiw->ki', stacked, activated, preferred_element_type=...  6.64 us
  transfers between devices with their start and end apart: 6, of which 5 were waited for; matrix products, arithmetic and copies ran while one was open for 11% of the time, Pallas kernels for 0%

commit v1 on v0

--- a/solution.py
+++ b/solution.py
@@ -2,6 +2,27 @@
 import jax.numpy as jnp
 from jax import lax
 from jax.sharding import PartitionSpec as P
+
+
+def ring_gather(array, axis, dim):
+    size, position, width = (lax.axis_size(axis), lax.axis_index(axis), array.shape[dim])
+    right = [(i, (i + 1) % size) for i in range(size)]
+    behind = [(i, (i - 1) % size) for i in range(size)]
+    result = jnp.zeros((*array.shape[:dim], size * width, *array.shape[dim + 1 :]), array.dtype)
+    result = lax.dynamic_update_slice_in_dim(result, array, position * width, axis=dim)
+    from_left = from_right = array
+    half = size // 2
+    for step in range(1, half + 1):
+        from_left = lax.ppermute(from_left, axis, right)
+        result = lax.dynamic_update_slice_in_dim(
+            result, from_left, (position - step) % size * width, axis=dim
+        )
+        if step < size - half:
+            from_right = lax.ppermute(from_right, axis, behind)
+            result = lax.dynamic_update_slice_in_dim(
+                result, from_right, (position + step) % size * width, axis=dim
+            )
+    return result
 
 
 def with_halo(cells, sides, width):
@@ -46,7 +67,7 @@
 def on_device(inputs, grad_out, weight):
     clip_count, frame_count, row_count, in_part, col_count = inputs.shape
     out_part = grad_out.shape[3]
-    gathered = lax.all_gather(inputs, "chan", axis=3, tiled=True)
+    gathered = ring_gather(inputs, "chan", 3)
     activated = jax.nn.silu(gathered.astype(jnp.float32)).astype(jnp.bfloat16)
     in_width = activated.shape[3]
     grad_rim = with_halo(grad_out, (("space", 2),), 1)

time: 260 us -> 281 us (1.081)
  local copies, waits for them, and re-layouts: 26.3 us -> 47.6 us
  waiting for transfers between devices: 187 us -> 182 us
  starting transfers between devices: 7.63 us -> 11.6 us
    unnamed x33 -> x31, local copies, waits for them, and re-layouts: 10.7 us -> 24.3 us
    all_gather x1 -> x0, waiting for transfers between devices: 8.09 us -> none  [on_device(): gathered = lax.all_gather(inputs, 'chan', axis=3, tiled=True)]
    dynamic_update_slice x0 -> x4, local copies, waits for them, and re-layouts: none -> 5.88 us  [the longest x2 2.48 us: ring_gather(): lax.dynamic_update_slice_in_dim(result, from_left, (position - step) % si...]
    ppermute x0 -> x3, starting transfers between devices: none -> 5.02 us  [the longest x2 3.99 us: ring_gather(): from_left = lax.ppermute(from_left, axis, right)]
    ppermute x0 -> x3, waiting for transfers between devices: none -> 3.88 us  [the longest x2 3.88 us: ring_gather(): from_left = lax.ppermute(from_left, axis, right)]
  transfers between devices with their start and end apart: 6 -> 8, of which waited for: 5 -> 4; matrix products, arithmetic and copies ran while one was open for 11% -> 20% of each run, Pallas kernels for 0% -> 0%
where the time goes in v1:
time: 281 us; the launch traced here: 280 us
  waiting for transfers between devices  182 us (65%)
  local copies, waits for them, and re-layouts  47.6 us (17%)
  matrix products  14.2 us (5%)
  between operations  13.8 us (5%)
  starting transfers between devices  11.6 us (4%)
  other arithmetic  10.9 us (4%)
    psum x1, waiting for transfers between devices, on_device(): summed = lax.psum(clip_summed, 'space')  132 us
    reduce_scatter x1, waiting for transfers between devices, on_device(): lax.psum_scatter(partial_value, 'chan', scatter_dimension=3, tiled=True)  38.5 us
    unnamed x31, local copies, waits for them, and re-layouts  24.3 us
    dot_general x2, local copies, waits for them, and re-layouts, on_device(): jnp.einsum('cthkw,cthiw->ki', stacked, activated, preferred_element_type=...  14.1 us
    dot_general x1, matrix products, on_device(): jnp.einsum('cthkw,ki->cthiw', stacked, flat_kernel, preferred_element_typ...  7.54 us
    reduce_scatter x1, waiting for transfers between devices, on_device(): lax.psum_scatter(local_weight, 'rep', scatter_dimension=3, tiled=True)  7.36 us
    dot_general x1, matrix products, on_device(): jnp.einsum('cthkw,cthiw->ki', stacked, activated, preferred_element_type=...  6.64 us
  transfers between devices with their start and end apart: 8, of which 4 were waited for; matrix products, arithmetic and copies ran while one was open for 20% of the time, Pallas kernels for 0%

profile of v1, /device:TPU:0, one launch (start us, length us, event | category | flops | bytes accessed | tf_op | source)
XLA Modules:
  0.0 280.3 jit_solution(15691982863946229920)
XLA Ops:
  7.2 0.0 copy-start
  7.2 0.0 reduce-scatter.5.cloned.1.call-start
  7.2 3.0 %collective-permute-start.2 = (bf16[1,2,4,128,128]{4,3,2,1,0:T(8,128)(2,1)}, bf16[1,2,4,128,128]{4,3,2,1,0:T(8,128)(2,1)}, u32[]{:S(2)}, u32[]{:S(2)}) collective-permute-start(bf16[1,2,4,128,128]{4,3,2,1,0:T(8,128)(2,1)} %param.3), channel_id=1, source_target_pairs={{0,8},{8,16},{16,24},{24,0},{1,9},{9,17},{17,25},{25,1},{2,10},{10... | collective-permute-start | bytes 786440 | tf_op jit(solution)/shard_map/ppermute | solution.py:16
  10.2 1.0 collective-permute-start.3
  11.2 1.8 copy.18
  13.0 1.5 fusion.34
  14.6 1.3 collective-permute-start.1
  15.9 5.2 %collective-permute-start = (bf16[1,2,1,128,128]{3,4,2,1,0:T(8,128)(2,1)}, bf16[1,2,1,128,128]{3,4,2,1,0:T(8,128)(2,1)}, u32[]{:S(2)}, u32[]{:S(2)}) collective-permute-start(bf16[1,2,1,128,128]{3,4,2,1,0:T(8,128)(2,1)} %get-tuple-element.6), channel_id=1, source_target_pairs={{0,2},{2,4},{4,6},{1,3},{3,5},{5,7},{8,10},{10,12},{12,14},{9,11},... | collective-permute-start | bytes 196616 | tf_op jit(solution)/shard_map/ppermute | solution.py:36
  21.0 0.8 broadcast_dynamic-update-slice_fusion.7
  21.8 0.8 broadcast_dynamic-update-slice_fusion.6
  22.6 0.7 broadcast_dynamic-update-slice_fusion.5
  23.3 0.8 broadcast_dynamic-update-slice_fusion.4
  24.1 0.8 broadcast_dynamic-update-slice_fusion.3
  24.9 0.8 broadcast_dynamic-update-slice_fusion.2
  25.6 0.8 broadcast_dynamic-update-slice_fusion.1
  26.4 0.8 broadcast_dynamic-update-slice_fusion
  27.2 1.1 broadcast_in_dim.3
  28.3 1.7 copy_dynamic-update-slice_fusion.3
  30.0 0.8 broadcast_dynamic-update-slice_fusion.8
  30.8 0.0 collective-permute-done.1
  30.8 0.0 collective-permute-done
  30.8 1.2 fusion.21
  32.0 0.8 slice_dynamic-update-slice_fusion.14
  32.8 0.9 slice_dynamic-update-slice_fusion.13
  33.6 0.8 slice_dynamic-update-slice_fusion.12
  34.4 0.9 slice_dynamic-update-slice_fusion.11
  35.2 0.8 slice_dynamic-update-slice_fusion.10
  36.0 0.7 slice_dynamic-update-slice_fusion.9
  36.8 0.8 slice_dynamic-update-slice_fusion.8
  37.6 0.8 slice_dynamic-update-slice_fusion.7
  38.4 0.8 slice_dynamic-update-slice_fusion.6
  39.1 0.8 slice_dynamic-update-slice_fusion.5
  40.0 1.7 fusion.32
  41.7 0.8 slice_dynamic-update-slice_fusion.4
  42.5 0.8 slice_dynamic-update-slice_fusion.3
  43.4 0.0 copy-done.1
  43.4 0.8 constant_dynamic-update-slice_fusion
  44.1 0.8 slice_dynamic-update-slice_fusion.2
  44.9 0.8 slice_dynamic-update-slice_fusion.1
  45.7 1.6 fusion.31
  47.3 0.7 slice_dynamic-update-slice_fusion
  48.0 10.3 %copy.25 = bf16[3456,4,2,128]{3,0,2,1:T(8,128)(2,1)} copy(bf16[3456,4,2,128]{0,3,1,2:T(8,128)(2,1)} %bitcast.32) | data formatting | bytes 14155776 | tf_op jit(solution)/shard_map/cthkw,cthiw->ki/dot_general | solution.py:76
  58.4 0.0 collective-permute-done.2
  58.4 1.0 collective-permute-start.4
  59.4 1.7 copy_dynamic-update-slice_fusion.2
  61.1 0.0 collective-permute-done.3
  61.1 1.7 copy_dynamic-update-slice_fusion.1
  62.8 3.9 %collective-permute-done.4 = bf16[1,2,4,128,128]{4,3,2,1,0:T(8,128)(2,1)S(1)} collective-permute-done((bf16[1,2,4,128,128]{4,3,2,1,0:T(8,128)(2,1)}, bf16[1,2,4,128,128]{4,3,2,1,0:T(8,128)(2,1)S(1)}, u32[]{:S(2)}, u32[]{:S(2)}) %collective-permute-start.4) | collective-permute-done | bytes 262176 | tf_op jit(solution)/shard_map/ppermute | solution.py:16
  66.7 0.7 copy_dynamic-update-slice_fusion
  67.4 6.6 %fusion = f32[3,3,3,128,512,1,1]{4,3,0,1,2,6,5:T(8,128)S(1)} fusion(bf16[3,3,3,128,4,2,128]{6,3,2,1,0,5,4:T(8,128)(2,1)} %bitcast.33, bf16[1,2,4,512,128]{4,3,1,2,0:T(8,128)(2,1)} %copy_dynamic-update-slice_fusion), kind=kOutput, calls=%fused_computation | convolution fusion | flops 3627024384 | bytes 15204352 | tf_op jit(solution)/shard_map/cthkw,cthiw->ki/dot_general | solution.py:76
  74.1 3.7 %copy.44 = f32[3,3,3,128,512,1,1]{4,3,2,1,0,5,6:T(8,128)} copy(f32[3,3,3,128,512,1,1]{4,3,0,1,2,6,5:T(8,128)S(1)} %fusion) | data formatting | bytes 14155776 | tf_op jit(solution)/shard_map/cthkw,cthiw->ki/dot_general | solution.py:76
  77.8 0.0 reduce-scatter.5.cloned.1.call-update
  77.8 0.0 reduce-scatter.3.cloned.1.call-start
  77.9 7.5 %fusion.13 = f32[1,2,4,512,128]{3,4,2,1,0:T(8,128)} fusion(bf16[3456,512,1,1]{1,0,3,2:T(8,128)(2,1)S(1)} %bitcast.30, bf16[1,2,4,3456,128]{3,4,2,1,0:T(8,128)(2,1)} %slice_dynamic-update-slice_fusion), kind=kOutput, calls=%fused_computation.20 | convolution fusion | flops 3623878656 | bytes 12713984 | tf_op jit(solution)/shard_map/cthkw,ki->cthiw/dot_general | solution.py:84
  85.4 0.0 reduce-scatter.3.cloned.1.call-update
  85.5 0.0 all-reduce.3.cloned.1.call-start
  85.5 7.4 %reduce-scatter.5.cloned.1.call-done = f32[3,3,3,64,512]{4,3,2,1,0:T(8,128)} async-done(((f32[3,3,3,128,512]{4,3,2,1,0:T(8,128)}), f32[3,3,3,64,512]{4,3,2,1,0:T(8,128)}) %reduce-scatter.5.cloned.1.call-update) | async-done | bytes 3538960 | tf_op jit(solution)/shard_map/reduce_scatter | solution.py:80
  92.9 0.0 all-reduce.3.cloned.1.call-update
  92.9 1.8 copy.24
  94.7 38.5 %reduce-scatter.3.cloned.1.call-done = f32[1,2,4,128,128]{3,4,2,1,0:T(8,128)} async-done(((f32[1,2,4,512,128]{3,4,2,1,0:T(8,128)}), f32[1,2,4,128,128]{3,4,2,1,0:T(8,128)}) %reduce-scatter.3.cloned.1.call-update) | async-done | bytes 524304 | tf_op jit(solution)/shard_map/reduce_scatter | solution.py:87
  133.1 2.0 fusion.30
  135.1 1.8 copy.31
  136.9 132.4 %all-reduce.3.cloned.1.call-done = f32[3,3,3,64,512]{4,3,2,1,0:T(8,128)} async-done(((f32[3,3,3,64,512]{4,3,2,1,0:T(8,128)}), f32[3,3,3,64,512]{4,3,2,1,0:T(8,128)}) %all-reduce.3.cloned.1.call-update) | async-done | bytes 3538960 | tf_op jit(solution)/shard_map/psum | solution.py:81
  269.3 4.4 %broadcast_multiply_fusion = f32[3,3,3,64,512]{4,3,2,1,0:T(8,128)} fusion(f32[3,3,3,64,512]{4,3,2,1,0:T(8,128)} %all-reduce.3.cloned.1.call-done), kind=kLoop, calls=%fused_computation.13 | loop fusion | flops 884736 | bytes 7077888 | tf_op jit(solution)/shard_map/mul | solution.py:82
  (2 shorter events, 0.0 us)
Async XLA Ops:
  7.2 70.7 %copy-start = (bf16[3,3,3,128,512]{4,3,2,1,0:T(8,128)(2,1)S(1)}, bf16[3,3,3,128,512]{4,3,2,1,0:T(8,128)(2,1)}, u32[]{:S(2)}) copy-start(bf16[3,3,3,128,512]{4,3,2,1,0:T(8,128)(2,1)} %param.5) | copy-start | bytes 10616836
  7.2 85.7 %reduce-scatter.5.cloned.1.call-start = ((), (), s32[]{:S(2)}) async-start(), calls=%async_computation.3 | async-start | bytes 10616832 | tf_op jit(solution)/shard_map/reduce_scatter | solution.py:80
  7.2 51.1 %collective-permute-start.2 = (bf16[1,2,4,128,128]{4,3,2,1,0:T(8,128)(2,1)}, bf16[1,2,4,128,128]{4,3,2,1,0:T(8,128)(2,1)}, u32[]{:S(2)}, u32[]{:S(2)}) collective-permute-start(bf16[1,2,4,128,128]{4,3,2,1,0:T(8,128)(2,1)} %param.3), channel_id=1, source_target_pairs={{0,8},{8,16},{16,24},{24,0},{1,9},{9,17},{17,25},{25,1},{2,10},{10... | collective-permute-start | bytes 786440 | tf_op jit(solution)/shard_map/ppermute | solution.py:16
  10.2 50.9 %collective-permute-start.3 = (bf16[1,2,4,128,128]{4,3,2,1,0:T(8,128)(2,1)}, bf16[1,2,4,128,128]{4,3,2,1,0:T(8,128)(2,1)}, u32[]{:S(2)}, u32[]{:S(2)}) collective-permute-start(bf16[1,2,4,128,128]{4,3,2,1,0:T(8,128)(2,1)} %param.3), channel_id=1, source_target_pairs={{0,24},{8,0},{16,8},{24,16},{1,25},{9,1},{17,9},{25,17},{2,26},{10... | collective-permute-start | bytes 786440 | tf_op jit(solution)/shard_map/ppermute | solution.py:21
  14.6 16.3 %collective-permute-start.1 = (bf16[1,2,1,128,128]{3,4,2,1,0:T(8,128)(2,1)}, bf16[1,2,1,128,128]{3,4,2,1,0:T(8,128)(2,1)}, u32[]{:S(2)}, u32[]{:S(2)}) collective-permute-start(bf16[1,2,1,128,128]{3,4,2,1,0:T(8,128)(2,1)} %get-tuple-element.7), channel_id=1, source_target_pairs={{2,0},{4,2},{6,4},{3,1},{5,3},{7,5},{10,8},{12,10},{14,12},{11,9},... | collective-permute-start | bytes 196616 | tf_op jit(solution)/shard_map/ppermute | solution.py:38
  15.9 15.0 %collective-permute-start = (bf16[1,2,1,128,128]{3,4,2,1,0:T(8,128)(2,1)}, bf16[1,2,1,128,128]{3,4,2,1,0:T(8,128)(2,1)}, u32[]{:S(2)}, u32[]{:S(2)}) collective-permute-start(bf16[1,2,1,128,128]{3,4,2,1,0:T(8,128)(2,1)} %get-tuple-element.6), channel_id=1, source_target_pairs={{0,2},{2,4},{4,6},{1,3},{3,5},{5,7},{8,10},{10,12},{12,14},{9,11},... | collective-permute-start | bytes 196616 | tf_op jit(solution)/shard_map/ppermute | solution.py:36
  30.0 13.3 %copy-start.1 = (bf16[1,2,4,128,128]{3,4,2,1,0:T(8,128)(2,1)S(1)}, bf16[1,2,4,128,128]{3,4,2,1,0:T(8,128)(2,1)}, u32[]{:S(2)}) copy-start(bf16[1,2,4,128,128]{3,4,2,1,0:T(8,128)(2,1)} %copy.18) | copy-start | bytes 786436
  58.4 8.3 %collective-permute-start.4 = (bf16[1,2,4,128,128]{4,3,2,1,0:T(8,128)(2,1)}, bf16[1,2,4,128,128]{4,3,2,1,0:T(8,128)(2,1)S(1)}, u32[]{:S(2)}, u32[]{:S(2)}) collective-permute-start(bf16[1,2,4,128,128]{4,3,2,1,0:T(8,128)(2,1)} %collective-permute-done.2), channel_id=1, source_target_pairs={{0,8},{8,16},{16,24},{24,0},{1,9},{9,17},{17,25},{25,1},{2,10},{10... | collective-permute-start | bytes 786440 | tf_op jit(solution)/shard_map/ppermute | solution.py:16
  77.8 55.3 %reduce-scatter.3.cloned.1.call-start = ((), (), s32[]{:S(2)}) async-start(), calls=%async_computation.2 | async-start | bytes 2621440 | tf_op jit(solution)/shard_map/reduce_scatter | solution.py:87
  85.5 183.9 %all-reduce.3.cloned.1.call-start = ((), (), s32[]{:S(2)}) async-start(), calls=%async_computation.4 | async-start | bytes 7077888 | tf_op jit(solution)/shard_map/psum | solution.py:81
Sparse Core Ops, SparseCore 0:
  77.9 14.8 reduce-scatter.4
  96.7 36.4 reduce-scatter.2
  135.5 133.7 all-reduce.2
